TPU v7x, 128 devices: a whole 4x4x4 slice. The times are simulated.
128 devices in a mesh: pool: 8 (over x, core), wide: 8 (over y, z_hi), narrow: 2 (over z_lo).
Axes of the slice: x: 4, y: 4, z: 4 (z_hi: 2, z_lo: 2; z = z_hi * 2 + z_lo), core: 2. Of those that a mesh axis runs over, the one named last changes fastest.
Arguments:
- states: bfloat16 [384, 2560], P('pool'), may hold values from -3 to 3
- gain_in: float32 [2560], replicated, may hold values from 0.1 to 1.9
- w_qkv: bfloat16 [2560, 8, 6, 128], P('narrow', 'wide'), may hold values from -0.125 to 0.125
- q_gain: float32 [128], replicated, may hold values from 0.1 to 1.9
- k_gain: float32 [128], replicated, may hold values from 0.1 to 1.9
- key_cache: bfloat16 [2304, 8, 128, 128], P('pool', 'wide', 'narrow'), as said below
- value_cache: bfloat16 [2304, 8, 128, 128], P('pool', 'wide', 'narrow'), may hold values from -12 to 12
- cache_len: int32 [384], replicated, may hold values from 1 to 8192, as said below
- page_table: int32 [384, 64], replicated, may hold values from -1 to 2303, as said below
- w_out: bfloat16 [4096, 2560], P('wide'), may hold values from -0.125 to 0.125
- gain_post: float32 [2560], replicated, may hold values from 0.1 to 1.9
- w_gate_up: bfloat16 [2560, 2, 9728], P(None, None, ('wide', 'narrow')), may hold values from -0.125 to 0.125
- w_down: bfloat16 [9728, 2560], P(('wide', 'narrow')), may hold values from -0.078125 to 0.078125
Outputs:
- attn_mixed: bfloat16 [384, 2560], P('pool')
- layer_out: bfloat16 [384, 2560], P('pool')
Inputs may be any that keep to these rules, and one draw needn't show every extreme that they name: `cache_len`: exactly one request has 8192 cached tokens; every other request has at most (5) * 128. `page_table`: entry (r, b) is pool device times 288 plus slot of the page with tokens b * 128 to (b + 1) * 128 - 1 of request r for b < ceil(cache_len[r] / 128), and -1 for later b; no slot is named twice. One pool device holds exactly 288 pages; the others hold the remaining pages, within one page of each other. `key_cache`: cached keys.
All inputs are finite; a program needn't handle non-finite values.
Results may differ from a plain program's by a relative error of at most 0.012.
The roundings to bfloat16 on the way count: a program that leaves them out, or rounds other values in their place, can miss the bound.
Values may be sent and summed in bfloat16 or wider, within the bound.
No kernel may reach another device: no remote copies, remote signals or barrier semaphores. Data moves between devices by JAX's collectives and lax.ppermute only.
A program may use at most 128 MiB of HBM per device.

v0:
```python
import math
import jax
import jax.numpy as jnp
from jax import lax
from jax.sharding import PartitionSpec as P

epsilon = 1e-06
rope_base = 1000000.0
masked_score = -1e30


def rms_scale(values, gain):
    return values * lax.rsqrt(jnp.mean(values * values, axis=-1, keepdims=True) + epsilon) * gain


def rotate(values, angle_pos):
    half = values.shape[-1] // 2
    ramp = jnp.arange(half).astype(jnp.float32)
    freqs = jnp.exp(ramp * (-2.0 * math.log(rope_base) / values.shape[-1]))
    angle = angle_pos[..., None] * freqs
    cosine = jnp.cos(angle)
    sine = jnp.sin(angle)
    lower = values[..., :half]
    upper = values[..., half:]
    return jnp.concatenate([lower * cosine - upper * sine, upper * cosine + lower * sine], axis=-1)


def feed_forward(normed_post, w_gate_up):
    gate_up = jnp.einsum("rd,dcf->rcf", normed_post, w_gate_up, preferred_element_type=jnp.float32)
    return (jax.nn.silu(gate_up[:, 0]) * gate_up[:, 1]).astype(jnp.bfloat16)


def per_device(
    states,
    gain_in,
    w_qkv,
    q_gain,
    k_gain,
    key_cache,
    value_cache,
    cache_len,
    page_table,
    w_out,
    gain_post,
    w_gate_up,
    w_down,
):
    kv_local = w_qkv.shape[1]
    group = w_qkv.shape[2] - 2
    head_dim = w_qkv.shape[3]
    scale = head_dim ** (-0.5)
    narrow_size = lax.axis_size("narrow")
    narrow_index = lax.axis_index("narrow")
    pool_index = lax.axis_index("pool")
    resid_in = states.astype(jnp.float32)
    normed = rms_scale(resid_in, gain_in).astype(jnp.bfloat16)
    part_width = w_qkv.shape[0]
    own_part = lax.dynamic_slice_in_dim(normed, narrow_index * part_width, part_width, 1)
    partial_proj = jnp.einsum("rd,dkch->rkch", own_part, w_qkv, preferred_element_type=jnp.float32)
    proj = lax.psum_scatter(partial_proj, "narrow", scatter_dimension=0, tiled=True)
    row_count = proj.shape[0]
    first_row = (pool_index * narrow_size + narrow_index) * row_count
    own_len = lax.dynamic_slice_in_dim(cache_len, first_row, row_count, 0)
    position = own_len.astype(jnp.float32)
    query = rotate(
        rms_scale(proj[:, :, :group], q_gain),
        jnp.broadcast_to(position[:, None, None], (row_count, kv_local, group)),
    ).astype(jnp.bfloat16)
    key_new = rotate(rms_scale(proj[:, :, group], k_gain), position[:, None]).astype(jnp.bfloat16)
    value_new = proj[:, :, group + 1].astype(jnp.bfloat16)
    all_queries = lax.all_gather(query, ("pool", "narrow"), axis=0, tiled=True)
    slot_count = key_cache.shape[0]
    half_page = key_cache.shape[2]
    holder_count = lax.axis_size("pool")
    req_count = page_table.shape[0]
    max_blocks = page_table.shape[1]
    flat_pages = page_table.reshape(-1)
    entry = jnp.arange(req_count * max_blocks, dtype=jnp.int32)
    target = jnp.where(flat_pages >= 0, flat_pages, holder_count * slot_count)
    owner_all = (
        jnp.full((holder_count * slot_count,), -1, jnp.int32)
        .at[target]
        .set(entry // max_blocks, mode="drop")
    )
    block_all = (
        jnp.zeros((holder_count * slot_count,), jnp.int32)
        .at[target]
        .set(entry % max_blocks, mode="drop")
    )
    owner = lax.dynamic_slice_in_dim(owner_all, pool_index * slot_count, slot_count, 0)
    block = lax.dynamic_slice_in_dim(block_all, pool_index * slot_count, slot_count, 0)
    safe_owner = jnp.maximum(owner, 0)
    page_len = half_page * narrow_size
    token_pos = (
        block[:, None] * page_len
        + narrow_index * half_page
        + jnp.arange(half_page, dtype=jnp.int32)[None, :]
    )
    live = (owner[:, None] >= 0) & (token_pos < cache_len[safe_owner][:, None])
    live_mask = live[:, None, None, :]
    slot_query = all_queries[safe_owner]
    scores = (
        jnp.einsum("skgd,sktd->skgt", slot_query, key_cache, preferred_element_type=jnp.float32)
        * scale
    )
    slot_top = jnp.max(jnp.where(live_mask, scores, masked_score), axis=-1)
    member = owner[:, None] == jnp.arange(req_count, dtype=jnp.int32)[None, :]
    req_top = jnp.max(jnp.where(member[:, :, None, None], slot_top[:, None], masked_score), axis=0)
    expo = jnp.where(live_mask, jnp.exp(scores - req_top[safe_owner][..., None]), 0.0)
    slot_total = jnp.sum(expo, axis=-1)
    slot_out = jnp.einsum(
        "skgt,sktd->skgd",
        expo.astype(jnp.bfloat16),
        value_cache,
        preferred_element_type=jnp.float32,
    )
    member_weight = member.astype(jnp.float32)
    req_out = jnp.einsum(
        "sr,sx->rx",
        member_weight,
        slot_out.reshape(slot_count, -1),
        precision=lax.Precision.HIGHEST,
    )
    req_out = req_out.reshape(req_count, kv_local, group, head_dim)
    req_total = jnp.einsum(
        "sr,sx->rx",
        member_weight,
        slot_total.reshape(slot_count, -1),
        precision=lax.Precision.HIGHEST,
    )
    req_total = req_total.reshape(req_count, kv_local, group)
    got_out, got_top, got_total = (
        lax.all_to_all(req_out[None], ("pool", "narrow"), split_axis=1, concat_axis=0, tiled=True),
        lax.all_to_all(req_top[None], ("pool", "narrow"), split_axis=1, concat_axis=0, tiled=True),
        lax.all_to_all(
            req_total[None], ("pool", "narrow"), split_axis=1, concat_axis=0, tiled=True
        ),
    )
    own_score = (
        jnp.einsum("rkgd,rkd->rkg", query, key_new, preferred_element_type=jnp.float32) * scale
    )
    top = jnp.maximum(jnp.max(got_top, axis=0), own_score)
    factor = jnp.exp(got_top - top[None])
    own_expo = jnp.exp(own_score - top)
    total = jnp.sum(got_total * factor, axis=0) + own_expo
    own_term = jnp.einsum(
        "rkg,rkd->rkgd",
        own_expo.astype(jnp.bfloat16),
        value_new,
        preferred_element_type=jnp.float32,
    )
    summed = jnp.sum(got_out * factor[..., None], axis=0) + own_term
    attn = (
        (summed / total[..., None])
        .astype(jnp.bfloat16)
        .reshape(row_count, kv_local * group * head_dim)
    )
    partial_out = jnp.dot(
        lax.all_gather(attn, "narrow", axis=0, tiled=True),
        w_out,
        preferred_element_type=jnp.float32,
    )
    mixed = lax.psum(partial_out, "wide")
    resid = resid_in + mixed
    attn_mixed = mixed.astype(jnp.bfloat16)
    normed_post = rms_scale(resid, gain_post).astype(jnp.bfloat16)
    hidden = feed_forward(normed_post, w_gate_up)
    down = jnp.dot(hidden, w_down, preferred_element_type=jnp.float32)
    layer_out = (resid + lax.psum(down, ("wide", "narrow"))).astype(jnp.bfloat16)
    return (attn_mixed, layer_out)


def solution(mesh):
    in_specs = (
        P("pool", None),
        P(),
        P("narrow", "wide", None, None),
        P(),
        P(),
        P("pool", "wide", "narrow", None),
        P("pool", "wide", "narrow", None),
        P(),
        P(),
        P("wide", None),
        P(),
        P(None, None, ("wide", "narrow")),
        P(("wide", "narrow"), None),
    )
    out_specs = (P("pool", None), P("pool", None))
    return jax.shard_map(
        per_device, mesh=mesh, in_specs=in_specs, out_specs=out_specs, check_vma=False
    )
```

profile of v0, /device:TPU:0, one launch (start us, length us, event | category | flops | bytes accessed | tf_op | source)
XLA Modules:
  0.0 489.5 jit_solution(1775987561983351854)
XLA Ops:
  7.2 1.2 multiply_reduce_fusion.1
  8.5 1.8 convert_element_type.67
  10.3 0.8 dynamic-slice
  11.0 2.9 fusion.9
  14.0 0.7 fusion.32
  15.1 90.5 %scatter_custom_fusion.1 = s32[2304]{0:T(1024)S(1)} fusion(s32[24576]{0:T(1024)S(1)} %bitcast.105, s32[24576]{0:T(1024)} %fusion.32, s32[]{:T(128)} %constant.29.clone.1), kind=kCustom, calls=%fused_computation.110 | custom fusion | bytes 9728 | tf_op jit(solution)/shard_map/scatter | solution.py:88
  105.6 90.2 %scatter_custom_fusion = s32[2304]{0:T(1024)S(1)} fusion(s32[24576]{0:T(1024)S(1)} %bitcast.106, s32[24576]{0:T(1024)S(1)} %add_select_fusion, s32[]{:T(128)} %constant.28.clone.1), kind=kCustom, calls=%fused_computation.112 | custom fusion | bytes 9220 | tf_op jit(solution)/shard_map/scatter | solution.py:83
  196.0 2.4 gather_fusion
  198.7 0.8 iota_compare_fusion
  199.5 0.8 multiply_reduce_fusion.4
  200.3 0.9 multiply_reduce_fusion.3
  201.2 0.8 multiply_multiply_fusion.1
  202.0 0.7 fusion.76
  202.8 0.9 multiply_multiply_fusion
  203.9 32.0 %all_gather.6 = bf16[384,1,4,128]{3,0,2,1:T(8,128)(2,1)S(1)} all-gather(bf16[24,1,4,128]{3,0,2,1:T(8,128)(2,1)S(1)} %pad_maximum_fusion), channel_id=1, replica_groups=mesh['pool'=8,'wide'=8,'narrow'=2] {'pool','narrow'}, dimensions={0}, use_global_device_ids=true | all-gather | bytes 417792 | tf_op jit(solution)/shard_map/all_gather | solution.py:71
  236.2 2.4 gather_fusion.1
  238.6 5.8 %select_reduce_fusion.1 = (f32[288,4]{1,0:T(8,128)S(1)}, f32[288,4,64]{2,1,0:T(4,128)}) fusion(pred[288,64]{1,0:T(8,128)(4,1)S(1)} %fusion.36, bf16[288,4,128]{2,1,0:T(4,128)(2,1)} %gather_fusion.1, bf16[288,1,64,128]{3,2,1,0:T(8,128)(2,1)} %param.18), kind=kOutput, calls=%fused_computation.23 | convolution fusion | flops 19094400 | bytes 5331456 | tf_op jit(solution)/shard_map/skgd,sktd->skgt/dot_general | solution.py:103
  245.0 0.8 copy.68
  245.8 3.5 all-to-all-start.1
  249.3 1.7 gather_fusion.2
  251.1 1.9 fusion.16
  253.0 4.8 fusion
  257.9 1.4 fusion.29
  259.5 0.8 fusion.58
  260.2 1.3 fusion.70
  261.5 5.6 %all-to-all-start.2 = ((f32[1,384,1,4]{3,2,0,1:T(1,128)}), f32[1,384,1,4]{3,2,0,1:T(1,128)S(1)}, u32[]{:S(2)}, u32[]{:S(2)}) async-start(f32[1,384,1,4]{3,2,0,1:T(1,128)} %bitcast.101), calls=%async_computation.3 | async-start | bytes 393216 | tf_op jit(solution)/shard_map/all_to_all | solution.py:135
  267.2 2.0 convolution_bitcast_fusion
  269.1 1.4 copy.67
  270.5 0.6 reduce_max.32
  271.2 3.5 all-to-all-done.2
  274.7 0.7 copy-done.3
  275.4 4.3 all-to-all-start
  279.7 0.8 multiply_maximum_fusion
  281.1 0.7 subtract_exponential_fusion
  281.8 1.7 copy.69
  283.5 1.0 multiply_reduce_fusion.2
  284.5 0.7 convert_convert_fusion
  285.4 8.9 %all-to-all-done = f32[1,384,1,4,128]{4,3,2,0,1:T(4,128)} async-done(((f32[1,384,1,4,128]{4,3,2,0,1:T(4,128)}), f32[1,384,1,4,128]{4,3,2,0,1:T(4,128)}, u32[]{:S(2)}, u32[]{:S(2)}) %all-to-all-start) | async-done | bytes 786464 | tf_op jit(solution)/shard_map/all_to_all | solution.py:133
  294.3 1.4 fusion.12
  295.7 0.8 copy_bitcast_fusion
  296.5 4.5 all_gather.7
  301.0 3.1 fusion.81
  304.2 85.7 %all-reduce.3.cloned.1.call-done = f32[48,2560]{1,0:T(8,128)} async-done(((f32[48,2560]{1,0:T(8,128)}), f32[48,2560]{1,0:T(8,128)}) %all-reduce.3.cloned.1.call-update) | async-done | bytes 491536 | tf_op jit(solution)/shard_map/psum | solution.py:163
  389.9 1.2 multiply_reduce_fusion
  391.1 4.9 fusion.23
  396.1 1.4 fusion.50
  397.5 83.2 %all-reduce.5.cloned.1.call-done = f32[48,2560]{1,0:T(8,128)} async-done(((f32[48,2560]{1,0:T(8,128)}), f32[48,2560]{1,0:T(8,128)}) %all-reduce.5.cloned.1.call-update) | async-done | bytes 491536 | tf_op jit(solution)/shard_map/psum | solution.py:169
  480.8 2.2 add_convert_fusion
  (70 shorter events, 3.1 us)
Async XLA Ops:
  7.2 388.9 %copy-start = (bf16[608,2560]{1,0:T(8,128)(2,1)S(1)}, bf16[608,2560]{1,0:T(8,128)(2,1)}, u32[]{:S(2)}) copy-start(bf16[608,2560]{1,0:T(8,128)(2,1)} %param.25) | copy-start | bytes 9338884
  7.2 7.4 %copy-start.11 = (s32[384,64]{0,1:T(8,128)S(1)}, s32[384,64]{0,1:T(8,128)}, u32[]{:S(2)}) copy-start(s32[384,64]{0,1:T(8,128)} %param.21) | copy-start | bytes 294916
  7.2 188.8 %copy-start.1 = (s32[384]{0:T(512)S(1)}, s32[384]{0:T(512)}, u32[]{:S(2)}) copy-start(s32[384]{0:T(512)} %param.20) | copy-start | bytes 4612
  7.2 192.3 %reduce-scatter.2.cloned.1.call-start = ((), (), s32[]{:S(2)}) async-start(), calls=%async_computation.4 | async-start | bytes 221184 | tf_op jit(solution)/shard_map/reduce_scatter | solution.py:60
  10.3 192.5 %copy-start.18 = (f32[128]{0:T(128)S(1)}, f32[128]{0:T(128)}, u32[]{:S(2)}) copy-start(f32[128]{0:T(128)} %param.16) | copy-start | bytes 1540
  195.9 40.0 %copy-start.12 = (s32[288]{0:T(512)}, s32[288]{0:T(512)S(1)}, u32[]{:S(2)}) copy-start(s32[288]{0:T(512)S(1)} %get-tuple-element.3) | copy-start | bytes 3460
  195.9 48.5 %copy-start.14 = (s32[1024]{0:T(1024)}, s32[1024]{0:T(1024)S(1)}, u32[]{:S(2)}) copy-start(s32[1024]{0:T(1024)S(1)} %pad_clamp_fusion) | copy-start | bytes 12292
  198.6 45.8 %copy-start.5 = (pred[288,64]{1,0:T(8,128)(4,1)}, pred[288,64]{1,0:T(8,128)(4,1)S(1)}, u32[]{:S(2)}) copy-start(pred[288,64]{1,0:T(8,128)(4,1)S(1)} %fusion.36) | copy-start | bytes 55300
  203.8 32.1 %copy-start.6 = (bf16[24,1,4,64]{3,0,2,1:T(8,128)(2,1)}, bf16[24,1,4,64]{3,0,2,1:T(8,128)(2,1)S(1)}, u32[]{:S(2)}) copy-start(bf16[24,1,4,64]{3,0,2,1:T(8,128)(2,1)S(1)} %get-tuple-element.6) | copy-start | bytes 36868
  203.8 32.1 %copy-start.8 = (bf16[24,1,4,64]{3,0,2,1:T(8,128)(2,1)}, bf16[24,1,4,64]{3,0,2,1:T(8,128)(2,1)S(1)}, u32[]{:S(2)}) copy-start(bf16[24,1,4,64]{3,0,2,1:T(8,128)(2,1)S(1)} %get-tuple-element.7) | copy-start | bytes 36868
  238.6 5.9 %copy-start.4 = (pred[288,384]{1,0:T(8,128)(4,1)S(1)}, pred[288,384]{1,0:T(8,128)(4,1)}, u32[]{:S(2)}) copy-start(pred[288,384]{1,0:T(8,128)(4,1)} %iota_compare_fusion) | copy-start | bytes 331780
  245.8 15.7 %all-to-all-start.1 = ((f32[1,384,1,4]{3,2,0,1:T(1,128)}), f32[1,384,1,4]{3,2,0,1:T(1,128)S(1)}, u32[]{:S(2)}, u32[]{:S(2)}) async-start(f32[1,384,1,4]{3,2,0,1:T(1,128)} %copy.68), calls=%async_computation.2 | async-start | bytes 393216 | tf_op jit(solution)/shard_map/all_to_all | solution.py:134
  252.9 4.9 %copy-start.13 = (s32[288]{0:T(512)S(1)}, s32[288]{0:T(512)}, u32[]{:S(2)}) copy-start(s32[288]{0:T(512)} %copy-done.12) | copy-start | bytes 3460
  253.0 6.3 %copy-start.15 = (bf16[24,64]{1,0:T(8,128)(2,1)S(1)}, bf16[24,64]{1,0:T(8,128)(2,1)}, u32[]{:S(2)}) copy-start(bf16[24,64]{1,0:T(8,128)(2,1)} %get-tuple-element.10) | copy-start | bytes 9220
  253.0 6.3 %copy-start.16 = (bf16[24,64]{1,0:T(8,128)(2,1)S(1)}, bf16[24,64]{1,0:T(8,128)(2,1)}, u32[]{:S(2)}) copy-start(bf16[24,64]{1,0:T(8,128)(2,1)} %get-tuple-element.11) | copy-start | bytes 9220
  253.0 6.4 %copy-start.7 = (bf16[24,1,4,64]{3,0,2,1:T(8,128)(2,1)S(1)}, bf16[24,1,4,64]{3,0,2,1:T(8,128)(2,1)}, u32[]{:S(2)}) copy-start(bf16[24,1,4,64]{3,0,2,1:T(8,128)(2,1)} %copy-done.6) | copy-start | bytes 36868
  253.0 6.4 %copy-start.9 = (bf16[24,1,4,64]{3,0,2,1:T(8,128)(2,1)S(1)}, bf16[24,1,4,64]{3,0,2,1:T(8,128)(2,1)}, u32[]{:S(2)}) copy-start(bf16[24,1,4,64]{3,0,2,1:T(8,128)(2,1)} %copy-done.8) | copy-start | bytes 36868
  261.5 13.2 %all-to-all-start.2 = ((f32[1,384,1,4]{3,2,0,1:T(1,128)}), f32[1,384,1,4]{3,2,0,1:T(1,128)S(1)}, u32[]{:S(2)}, u32[]{:S(2)}) async-start(f32[1,384,1,4]{3,2,0,1:T(1,128)} %bitcast.101), calls=%async_computation.3 | async-start | bytes 393216 | tf_op jit(solution)/shard_map/all_to_all | solution.py:135
  274.7 0.7 copy-start.3
  275.4 19.0 %all-to-all-start = ((f32[1,384,1,4,128]{4,3,2,0,1:T(4,128)}), f32[1,384,1,4,128]{4,3,2,0,1:T(4,128)}, u32[]{:S(2)}, u32[]{:S(2)}) async-start(f32[1,384,1,4,128]{4,3,2,0,1:T(4,128)} %copy.67), calls=%async_computation.1 | async-start | bytes 1572864 | tf_op jit(solution)/shard_map/all_to_all | solution.py:133
  279.6 110.3 %copy-start.2 = (bf16[48,2560]{1,0:T(8,128)(2,1)S(1)}, bf16[48,2560]{1,0:T(8,128)(2,1)}, u32[]{:S(2)}) copy-start(bf16[48,2560]{1,0:T(8,128)(2,1)} %param.13) | copy-start | bytes 737284
  279.7 110.3 %all-reduce.3.cloned.1.call-start = ((), (), s32[]{:S(2)}) async-start(), calls=%async_computation.5 | async-start | bytes 983040 | tf_op jit(solution)/shard_map/psum | solution.py:163
  280.5 0.6 copy-start.10
  284.5 106.7 %copy-start.17 = (f32[2560]{0:T(1024)S(1)}, f32[2560]{0:T(1024)}, u32[]{:S(2)}) copy-start(f32[2560]{0:T(1024)} %param.23) | copy-start | bytes 30724
  304.2 176.6 %all-reduce.5.cloned.1.call-start = ((), (), s32[]{:S(2)}) async-start(), calls=%async_computation.6 | async-start | bytes 983040 | tf_op jit(solution)/shard_map/psum | solution.py:169
Sparse Core Ops, SparseCore 0:
  14.1 15.5 reduce-scatter.1
  304.3 85.5 all-reduce.2
  397.6 83.0 all-reduce.4
where the time goes:
time: 491 us; the launch traced here: 489 us
  local copies, waits for them, and re-layouts  194 us (40%)
  waiting for transfers between devices  181 us (37%)
  blocking collectives  36.5 us (7%)
  matrix products  27.1 us (6%)
  other arithmetic  22.4 us (5%)
  between operations  14.1 us (3%)
  starting transfers between devices  13.6 us (3%)
    scatter x1, local copies, waits for them, and re-layouts, per_device(): block_all = jnp.zeros((holder_count * slot_count,), jnp.int32).at[target]...  90.5 us
    scatter x1, local copies, waits for them, and re-layouts, per_device(): owner_all = jnp.full((holder_count * slot_count,), -1, jnp.int32).at[targ...  90.2 us
    psum x1, waiting for transfers between devices, per_device(): mixed = lax.psum(partial_out, 'wide')  85.7 us
    psum x1, waiting for transfers between devices, per_device(): lax.psum(down, ('wide', 'narrow'))  83.2 us
    all_gather x1, blocking collectives, per_device(): all_queries = lax.all_gather(query, ('pool', 'narrow'), axis=0, tiled=True)  32 us
  transfers between devices with their start and end apart: 6, of which 4 were waited for; matrix products, arithmetic and copies ran while one was open for 42% of the time, Pallas kernels for 0%

commit v1 on v0

--- a/solution.py
+++ b/solution.py
@@ -68,7 +68,12 @@
     ).astype(jnp.bfloat16)
     key_new = rotate(rms_scale(proj[:, :, group], k_gain), position[:, None]).astype(jnp.bfloat16)
     value_new = proj[:, :, group + 1].astype(jnp.bfloat16)
-    all_queries = lax.all_gather(query, ("pool", "narrow"), axis=0, tiled=True)
+    all_queries = jnp.concatenate(
+        lax.all_to_all(
+            jnp.stack([query] * lax.axis_size(("pool", "narrow"))), ("pool", "narrow"), 0, 0
+        ),
+        axis=0,
+    )
     slot_count = key_cache.shape[0]
     half_page = key_cache.shape[2]
     holder_count = lax.axis_size("pool")

time: 491 us -> 475 us (0.967)
  blocking collectives: 36.5 us -> 4.5 us
  waiting for transfers between devices: 181 us -> 187 us
  starting transfers between devices: 13.6 us -> 19.4 us
    all_gather x1 -> x0, blocking collectives: 32 us -> none  [per_device(): all_queries = lax.all_gather(query, ('pool', 'narrow'), axis=0, tiled=True)]
    all_to_all x0 -> x1, waiting for transfers between devices: none -> 5.96 us  [per_device(): lax.all_to_all(jnp.stack([query] * lax.axis_size(('pool', 'narrow'))), ('...]
    all_to_all x0 -> x1, starting transfers between devices: none -> 5.83 us  [per_device(): lax.all_to_all(jnp.stack([query] * lax.axis_size(('pool', 'narrow'))), ('...]
  transfers between devices with their start and end apart: 6 -> 7, of which waited for: 4 -> 5; matrix products, arithmetic and copies ran while one was open for 42% -> 44% of each run, Pallas kernels for 0% -> 0%
where the time goes in v1:
time: 475 us; the launch traced here: 474 us
  local copies, waits for them, and re-layouts  195 us (41%)
  waiting for transfers between devices  187 us (39%)
  matrix products  27.8 us (6%)
  other arithmetic  24.9 us (5%)
  starting transfers between devices  19.4 us (4%)
  between operations  14 us (3%)
    scatter x1, local copies, waits for them, and re-layouts, per_device(): block_all = jnp.zeros((holder_count * slot_count,), jnp.int32).at[target]...  90.5 us
    scatter x1, local copies, waits for them, and re-layouts, per_device(): owner_all = jnp.full((holder_count * slot_count,), -1, jnp.int32).at[targ...  90.2 us
    psum x1, waiting for transfers between devices, per_device(): mixed = lax.psum(partial_out, 'wide')  85.7 us
    psum x1, waiting for transfers between devices, per_device(): lax.psum(down, ('wide', 'narrow'))  83.2 us
  transfers between devices with their start and end apart: 7, of which 5 were waited for; matrix products, arithmetic and copies ran while one was open for 44% of the time, Pallas kernels for 0%

profile of v1, /device:TPU:0, one launch (start us, length us, event | category | flops | bytes accessed | tf_op | source)
XLA Modules:
  0.0 473.6 jit_solution(7095109864976983266)
XLA Ops:
  7.2 1.2 multiply_reduce_fusion.1
  8.5 1.8 convert_element_type.66
  10.3 0.8 dynamic-slice
  11.0 2.9 fusion.9
  15.7 90.5 %scatter_custom_fusion.1 = s32[2304]{0:T(1024)S(1)} fusion(s32[24576]{0:T(1024)S(1)} %bitcast.106, s32[24576]{0:T(1024)} %fusion.32, s32[]{:T(128)} %constant.29.clone.1), kind=kCustom, calls=%fused_computation.110 | custom fusion | bytes 9728 | tf_op jit(solution)/shard_map/scatter | solution.py:93
  106.1 90.2 %scatter_custom_fusion = s32[2304]{0:T(1024)S(1)} fusion(s32[24576]{0:T(1024)S(1)} %bitcast.107, s32[24576]{0:T(1024)S(1)} %add_select_fusion, s32[]{:T(128)} %constant.28.clone.1), kind=kCustom, calls=%fused_computation.112 | custom fusion | bytes 9220 | tf_op jit(solution)/shard_map/scatter | solution.py:88
  196.6 2.4 gather_fusion
  199.3 0.8 iota_compare_fusion
  200.1 0.8 multiply_reduce_fusion.4
  200.9 0.9 multiply_reduce_fusion.3
  201.8 0.8 multiply_multiply_fusion.1
  202.6 1.4 fusion.77
  204.0 0.9 multiply_multiply_fusion
  204.9 0.8 fusion.59
  206.4 0.8 stack.2
  207.2 5.8 %all-to-all-start = ((bf16[16,24,1,4,128]{4,3,2,1,0:T(4,128)(2,1)}), bf16[16,24,1,4,128]{4,3,2,1,0:T(4,128)(2,1)S(1)}, u32[]{:S(2)}, u32[]{:S(2)}) async-start(bf16[16,24,1,4,128]{4,3,2,1,0:T(4,128)(2,1)} %stack.2), calls=%async_computation.1 | async-start | bytes 786432 | tf_op jit(solution)/shard_map/all_to_all | solution.py:72
  213.1 1.3 fusion.71
  214.4 0.8 maximum_bitcast_fusion
  215.1 1.5 fusion.68
  216.6 6.0 %all-to-all-done = bf16[16,24,1,4,128]{4,3,2,1,0:T(4,128)(2,1)S(1)} async-done(((bf16[16,24,1,4,128]{4,3,2,1,0:T(4,128)(2,1)}), bf16[16,24,1,4,128]{4,3,2,1,0:T(4,128)(2,1)S(1)}, u32[]{:S(2)}, u32[]{:S(2)}) %all-to-all-start) | async-done | bytes 393248 | tf_op jit(solution)/shard_map/all_to_all | solution.py:72
  222.6 2.4 gather_fusion.1
  225.0 5.8 %select_reduce_fusion.1 = (f32[288,4]{1,0:T(8,128)S(1)}, f32[288,4,64]{2,1,0:T(4,128)}) fusion(pred[288,64]{1,0:T(8,128)(4,1)S(1)} %fusion.36, bf16[288,4,128]{2,1,0:T(4,128)(2,1)} %gather_fusion.1, bf16[288,1,64,128]{3,2,1,0:T(8,128)(2,1)} %param.18), kind=kOutput, calls=%fused_computation.23 | convolution fusion | flops 19094400 | bytes 5331456 | tf_op jit(solution)/shard_map/skgd,sktd->skgt/dot_general | solution.py:108
  231.4 0.8 copy.68
  232.2 3.5 all-to-all-start.2
  235.7 1.7 gather_fusion.2
  237.5 1.9 fusion.16
  239.4 4.8 %fusion = f32[288,4,128]{2,1,0:T(4,128)} fusion(bf16[288,1,64,128]{3,2,1,0:T(8,128)(2,1)} %param.19, f32[288,4,64]{2,1,0:T(4,128)} %get-tuple-element.13, f32[288,4]{1,0:T(8,128)} %gather_fusion.2, pred[288,64]{1,0:T(8,128)(4,1)} %copy-done.5), kind=kOutput, calls=%fused_computation.5 | convolution fusion | flops 19095552 | bytes 5626368 | tf_op jit(solution)/shard_map/skgt,sktd->skgd/dot_general | solution.py:116
  244.2 1.4 fusion.29
  245.6 5.6 %all-to-all-start.3 = ((f32[1,384,1,4]{3,2,0,1:T(1,128)}), f32[1,384,1,4]{3,2,0,1:T(1,128)S(1)}, u32[]{:S(2)}, u32[]{:S(2)}) async-start(f32[1,384,1,4]{3,2,0,1:T(1,128)} %bitcast.104), calls=%async_computation.4 | async-start | bytes 393216 | tf_op jit(solution)/shard_map/all_to_all | solution.py:140
  251.3 2.0 convolution_bitcast_fusion
  253.3 1.4 copy.67
  255.3 3.5 all-to-all-done.3
  259.5 4.3 all-to-all-start.1
  263.8 0.8 multiply_maximum_fusion
  265.9 1.7 copy.69
  267.6 1.0 multiply_reduce_fusion.2
  268.6 0.7 convert_convert_fusion
  269.5 8.9 %all-to-all-done.1 = f32[1,384,1,4,128]{4,3,2,0,1:T(4,128)} async-done(((f32[1,384,1,4,128]{4,3,2,0,1:T(4,128)}), f32[1,384,1,4,128]{4,3,2,0,1:T(4,128)}, u32[]{:S(2)}, u32[]{:S(2)}) %all-to-all-start.1) | async-done | bytes 786464 | tf_op jit(solution)/shard_map/all_to_all | solution.py:138
  278.4 1.4 fusion.12
  279.9 0.8 copy_bitcast_fusion
  280.7 4.5 all_gather.3
  285.2 3.1 fusion.82
  288.3 85.7 %all-reduce.3.cloned.1.call-done = f32[48,2560]{1,0:T(8,128)} async-done(((f32[48,2560]{1,0:T(8,128)}), f32[48,2560]{1,0:T(8,128)}) %all-reduce.3.cloned.1.call-update) | async-done | bytes 491536 | tf_op jit(solution)/shard_map/psum | solution.py:168
  374.0 1.2 multiply_reduce_fusion
  375.3 4.9 %fusion.23 = f32[48,2,608]{2,0,1:T(8,128)S(1)} fusion(bf16[2560,2,608]{0,2,1:T(8,128)(2,1)} %param.24, f32[2560]{0:T(1024)S(1)} %copy-done.12, f32[48]{0:T(128)S(1)} %add_rsqrt_fusion.1, f32[48,2560]{1,0:T(8,128)} %all-reduce.3.cloned.1.call-done, bf16[48,2560]{1,0:T(8,128)(2,1)S(1)} %copy-done.2), kind=kOutput, calls=%fused_computation.36 | convolution fusion | flops 299458560 | bytes 7207104 | tf_op jit(solution)/shard_map/rd,dcf->rcf/dot_general | solution.py:29
  380.2 1.4 fusion.50
  381.6 83.2 %all-reduce.5.cloned.1.call-done = f32[48,2560]{1,0:T(8,128)} async-done(((f32[48,2560]{1,0:T(8,128)}), f32[48,2560]{1,0:T(8,128)}) %all-reduce.5.cloned.1.call-update) | async-done | bytes 491536 | tf_op jit(solution)/shard_map/psum | solution.py:174
  464.9 2.2 add_convert_fusion
  (61 shorter events, 6.4 us)
Async XLA Ops:
  7.2 373.0 %copy-start = (bf16[608,2560]{1,0:T(8,128)(2,1)S(1)}, bf16[608,2560]{1,0:T(8,128)(2,1)}, u32[]{:S(2)}) copy-start(bf16[608,2560]{1,0:T(8,128)(2,1)} %param.25) | copy-start | bytes 9338884
  7.2 8.0 %copy-start.8 = (s32[384,64]{0,1:T(8,128)S(1)}, s32[384,64]{0,1:T(8,128)}, u32[]{:S(2)}) copy-start(s32[384,64]{0,1:T(8,128)} %param.21) | copy-start | bytes 294916
  7.2 189.4 %copy-start.1 = (s32[384]{0:T(512)S(1)}, s32[384]{0:T(512)}, u32[]{:S(2)}) copy-start(s32[384]{0:T(512)} %param.20) | copy-start | bytes 4612
  7.2 192.9 %reduce-scatter.2.cloned.1.call-start = ((), (), s32[]{:S(2)}) async-start(), calls=%async_computation.5 | async-start | bytes 221184 | tf_op jit(solution)/shard_map/reduce_scatter | solution.py:60
  10.3 191.6 %copy-start.13 = (f32[128]{0:T(128)S(1)}, f32[128]{0:T(128)}, u32[]{:S(2)}) copy-start(f32[128]{0:T(128)} %param.17) | copy-start | bytes 1540
  196.5 10.8 %copy-start.9 = (s32[288]{0:T(512)}, s32[288]{0:T(512)S(1)}, u32[]{:S(2)}) copy-start(s32[288]{0:T(512)S(1)} %get-tuple-element.3) | copy-start | bytes 3460
  196.5 34.4 %copy-start.11 = (s32[1024]{0:T(1024)}, s32[1024]{0:T(1024)S(1)}, u32[]{:S(2)}) copy-start(s32[1024]{0:T(1024)S(1)} %pad_clamp_fusion) | copy-start | bytes 12292
  199.2 31.7 %copy-start.5 = (pred[288,64]{1,0:T(8,128)(4,1)}, pred[288,64]{1,0:T(8,128)(4,1)S(1)}, u32[]{:S(2)}) copy-start(pred[288,64]{1,0:T(8,128)(4,1)S(1)} %fusion.36) | copy-start | bytes 55300
  205.8 0.6 copy-start.7
  207.2 15.4 %all-to-all-start = ((bf16[16,24,1,4,128]{4,3,2,1,0:T(4,128)(2,1)}), bf16[16,24,1,4,128]{4,3,2,1,0:T(4,128)(2,1)S(1)}, u32[]{:S(2)}, u32[]{:S(2)}) async-start(bf16[16,24,1,4,128]{4,3,2,1,0:T(4,128)(2,1)} %stack.2), calls=%async_computation.1 | async-start | bytes 786432 | tf_op jit(solution)/shard_map/all_to_all | solution.py:72
  225.0 5.9 %copy-start.4 = (pred[288,384]{1,0:T(8,128)(4,1)S(1)}, pred[288,384]{1,0:T(8,128)(4,1)}, u32[]{:S(2)}) copy-start(pred[288,384]{1,0:T(8,128)(4,1)} %iota_compare_fusion) | copy-start | bytes 331780
  232.2 13.4 %all-to-all-start.2 = ((f32[1,384,1,4]{3,2,0,1:T(1,128)}), f32[1,384,1,4]{3,2,0,1:T(1,128)S(1)}, u32[]{:S(2)}, u32[]{:S(2)}) async-start(f32[1,384,1,4]{3,2,0,1:T(1,128)} %copy.68), calls=%async_computation.3 | async-start | bytes 393216 | tf_op jit(solution)/shard_map/all_to_all | solution.py:139
  239.4 4.8 %copy-start.10 = (s32[288]{0:T(512)S(1)}, s32[288]{0:T(512)}, u32[]{:S(2)}) copy-start(s32[288]{0:T(512)} %copy-done.9) | copy-start | bytes 3460
  245.6 13.2 %all-to-all-start.3 = ((f32[1,384,1,4]{3,2,0,1:T(1,128)}), f32[1,384,1,4]{3,2,0,1:T(1,128)S(1)}, u32[]{:S(2)}, u32[]{:S(2)}) async-start(f32[1,384,1,4]{3,2,0,1:T(1,128)} %bitcast.104), calls=%async_computation.4 | async-start | bytes 393216 | tf_op jit(solution)/shard_map/all_to_all | solution.py:140
  258.8 0.7 copy-start.3
  259.5 19.0 %all-to-all-start.1 = ((f32[1,384,1,4,128]{4,3,2,0,1:T(4,128)}), f32[1,384,1,4,128]{4,3,2,0,1:T(4,128)}, u32[]{:S(2)}, u32[]{:S(2)}) async-start(f32[1,384,1,4,128]{4,3,2,0,1:T(4,128)} %copy.67), calls=%async_computation.2 | async-start | bytes 1572864 | tf_op jit(solution)/shard_map/all_to_all | solution.py:138
  263.8 110.3 %copy-start.2 = (bf16[48,2560]{1,0:T(8,128)(2,1)S(1)}, bf16[48,2560]{1,0:T(8,128)(2,1)}, u32[]{:S(2)}) copy-start(bf16[48,2560]{1,0:T(8,128)(2,1)} %param.13) | copy-start | bytes 737284
  263.8 110.3 %all-reduce.3.cloned.1.call-start = ((), (), s32[]{:S(2)}) async-start(), calls=%async_computation.6 | async-start | bytes 983040 | tf_op jit(solution)/shard_map/psum | solution.py:168
  264.6 0.6 copy-start.6
  268.6 106.7 %copy-start.12 = (f32[2560]{0:T(1024)S(1)}, f32[2560]{0:T(1024)}, u32[]{:S(2)}) copy-start(f32[2560]{0:T(1024)} %param.23) | copy-start | bytes 30724
  288.3 176.6 %all-reduce.5.cloned.1.call-start = ((), (), s32[]{:S(2)}) async-start(), calls=%async_computation.7 | async-start | bytes 983040 | tf_op jit(solution)/shard_map/psum | solution.py:174
Sparse Core Ops, SparseCore 0:
  14.1 15.4 reduce-scatter.1
  288.4 85.5 all-reduce.2
  381.8 83.0 all-reduce.4
